TPU v7x, 32 devices: a whole 2x2x4 slice. The times are simulated.
32 devices in a mesh: ctx: 16 (over z, y, core), fsdp: 2 (over x).
Axes of the slice: x: 2, y: 2, z: 4, core: 2. Of those that a mesh axis runs over, the one named last changes fastest.
Arguments:
- tokens: bfloat16 [2, 2048, 1024], P('fsdp', 'ctx'), may hold values from -6 to 6
- w_qkv: bfloat16 [1024, 3072], P('fsdp'), may hold values from -0.1875 to 0.1875
- w_out: bfloat16 [1024, 1024], P('fsdp'), may hold values from -0.375 to 0.375
- w_up: bfloat16 [1024, 4096], P('fsdp'), may hold values from -0.1875 to 0.1875
- w_down: bfloat16 [4096, 1024], P('fsdp'), may hold values from -0.09375 to 0.09375
- w_time: bfloat16 [256, 2048], P('fsdp'), may hold values from -0.375 to 0.375
- gain_one: bfloat16 [1024], P('fsdp'), may hold values from 0.5 to 1.5
- bias_one: bfloat16 [1024], P('fsdp'), may hold values from -3 to 3
- gain_two: bfloat16 [1024], P('fsdp'), may hold values from 0.5 to 1.5
- bias_two: bfloat16 [1024], P('fsdp'), may hold values from -3 to 3
- bias_up: bfloat16 [4096], P('fsdp'), may hold values from -3 to 3
- bias_down: bfloat16 [1024], P('fsdp'), may hold values from -3 to 3
- lengths: int32 [2, 1], P('fsdp'), may hold values from 1024 to 2048, as said below
- time_steps: int32 [2, 1], P('fsdp'), may hold values from 0 to 999
- cotangent: bfloat16 [2, 2048, 1024], P('fsdp', 'ctx'), may hold values from -6 to 6
Outputs:
- output: bfloat16 [2, 2048, 1024], P('fsdp', 'ctx')
- grad_tokens: bfloat16 [2, 2048, 1024], P('fsdp', 'ctx')
- grad_qkv: float32 [1024, 3072], P('fsdp')
- grad_out: float32 [1024, 1024], P('fsdp')
- grad_up: float32 [1024, 4096], P('fsdp')
- grad_down: float32 [4096, 1024], P('fsdp')
- grad_time: float32 [256, 2048], P('fsdp')
- grad_gain_one: float32 [1024], P('fsdp')
- grad_bias_one: float32 [1024], P('fsdp')
- grad_gain_two: float32 [1024], P('fsdp')
- grad_bias_two: float32 [1024], P('fsdp')
- grad_bias_up: float32 [4096], P('fsdp')
- grad_bias_down: float32 [1024], P('fsdp')
Inputs may be any that keep to these rules, and one draw needn't show every extreme that they name: The 1 lengths of a group add up to at most 2048; the group's tokens after them are padding; in every group some sequence has the largest length.
All inputs are finite; a program needn't handle non-finite values.
Results may differ from a plain program's by a relative error of at most 0.025.
Values may be sent and summed in bfloat16 or wider, within the bound.
No kernel may reach another device: no remote copies, remote signals or barrier semaphores. Data moves between devices by JAX's collectives and lax.ppermute only.
A program may use at most 256 MiB of HBM per device.

v0:
```python
import math
import jax
import jax.numpy as jnp
from jax import lax
from jax.sharding import PartitionSpec as P

HEADS = 16
HIGH = lax.Precision.HIGHEST
EPSILON = 1e-05
NEGATIVE = -1e30


def layout(seq_lengths, offsets):
    ends = jnp.cumsum(seq_lengths)
    starts = jnp.concatenate([jnp.zeros((1,), jnp.int32), ends])
    segment = jnp.sum((offsets[:, None] >= ends[None, :]).astype(jnp.int32), axis=1)
    onehot = segment[:, None] == jnp.arange(seq_lengths.shape[0] + 1, dtype=jnp.int32)[None, :]
    begin = jnp.sum(jnp.where(onehot, starts[None, :], 0), axis=1)
    return (segment, onehot, offsets - begin)


def embed(steps_given, embed_width):
    half_width = embed_width // 2
    freq = jnp.exp(-math.log(10000.0) * jnp.arange(half_width, dtype=jnp.float32) / half_width)
    angle = steps_given.astype(jnp.float32)[..., None] * freq
    return jnp.concatenate([jnp.sin(angle), jnp.cos(angle)], axis=-1)


def rotary(values, position, heads):
    width = values.shape[-1]
    half_width = width // heads // 2
    inverse = jnp.exp(-math.log(10000.0) * jnp.arange(half_width, dtype=jnp.float32) / half_width)
    angle = position.astype(jnp.float32)[..., None] * inverse
    cosine = jnp.cos(angle)[..., None, :]
    sine = jnp.sin(angle)[..., None, :]
    split = values.reshape(values.shape[:-1] + (heads, 2, half_width))
    upper = split[..., 0, :]
    lower = split[..., 1, :]
    turned = jnp.stack([upper * cosine - lower * sine, lower * cosine + upper * sine], axis=-2)
    return turned.reshape(values.shape)


def normalize(values):
    centre = jnp.mean(values, axis=-1, keepdims=True)
    centered = values - centre
    spread = jnp.mean(centered * centered, axis=-1, keepdims=True)
    return centered * lax.rsqrt(spread + EPSILON)


def modulate(values, gain, bias, film_tok):
    width = values.shape[-1]
    return normalize(values) * (gain + film_tok[:, :width]) + (bias + film_tok[:, width:])


def affine(values, gain, bias):
    return normalize(values) * gain + bias


def gelu_exact(values):
    return jax.nn.gelu(values, approximate=False)


def split_heads(values, heads):
    return values.reshape(values.shape[0], heads, values.shape[1] // heads)


def contract_rows(left, right):
    return lax.dot_general(
        left, right, (((0,), (0,)), ((), ())), preferred_element_type=jnp.float32
    )


def contract_cols(left, right):
    return lax.dot_general(
        left, right, (((1,), (1,)), ((), ())), preferred_element_type=jnp.float32
    )


def body(
    tokens,
    w_qkv,
    w_out,
    w_up,
    w_down,
    w_time,
    gain_one,
    bias_one,
    gain_two,
    bias_two,
    bias_up,
    bias_down,
    lengths,
    time_steps,
    cotangent,
):
    gathered = (
        lax.all_gather(w_qkv, "fsdp", axis=0, tiled=True),
        lax.all_gather(w_out, "fsdp", axis=0, tiled=True),
        lax.all_gather(w_up, "fsdp", axis=0, tiled=True),
        lax.all_gather(w_down, "fsdp", axis=0, tiled=True),
        lax.all_gather(w_time, "fsdp", axis=0, tiled=True),
        lax.all_gather(gain_one, "fsdp", axis=0, tiled=True),
        lax.all_gather(bias_one, "fsdp", axis=0, tiled=True),
        lax.all_gather(gain_two, "fsdp", axis=0, tiled=True),
        lax.all_gather(bias_two, "fsdp", axis=0, tiled=True),
        lax.all_gather(bias_up, "fsdp", axis=0, tiled=True),
        lax.all_gather(bias_down, "fsdp", axis=0, tiled=True),
    )
    full_qkv, full_out, full_up, full_down, full_time = (
        gathered[0],
        gathered[1],
        gathered[2],
        gathered[3],
        gathered[4],
    )
    gain_first = gathered[5].astype(jnp.float32)
    bias_first = gathered[6].astype(jnp.float32)
    gain_second = gathered[7].astype(jnp.float32)
    bias_second = gathered[8].astype(jnp.float32)
    bias_hidden = gathered[9].astype(jnp.float32)
    bias_output = gathered[10].astype(jnp.float32)
    row_count = tokens.shape[1]
    width = tokens.shape[2]
    heads = HEADS
    head_size = width // heads
    scale = float(head_size) ** (-0.5)
    seq_lengths = lengths[0]
    seq_count = seq_lengths.shape[0]
    offsets = lax.axis_index("ctx") * row_count + jnp.arange(row_count, dtype=jnp.int32)
    segment, onehot, position = layout(seq_lengths, offsets)
    live = (segment < seq_count).astype(jnp.float32)
    onehot_float = onehot.astype(jnp.float32)
    inputs = tokens[0].astype(jnp.float32)
    temb = embed(time_steps[0], full_time.shape[0]).astype(jnp.bfloat16)
    film = jnp.dot(temb, full_time, preferred_element_type=jnp.float32)
    film_ext = jnp.concatenate([film, jnp.zeros((1, film.shape[1]), jnp.float32)], axis=0)
    film_tok = jnp.dot(onehot_float, film_ext, precision=HIGH)
    norm_one, pull_one = jax.vjp(modulate, inputs, gain_first, bias_first, film_tok)
    norm_one_b = norm_one.astype(jnp.bfloat16)
    mixed = jnp.dot(norm_one_b, full_qkv, preferred_element_type=jnp.float32)

    def turn_pair(query_raw, key_raw):
        return (rotary(query_raw, position, heads), rotary(key_raw, position, heads))

    turned, pull_turn = jax.vjp(turn_pair, mixed[:, :width], mixed[:, width : 2 * width])
    query = turned[0].astype(jnp.bfloat16)
    key = turned[1].astype(jnp.bfloat16)
    value = mixed[:, 2 * width :].astype(jnp.bfloat16)
    query_heads = split_heads(query, heads)
    key_heads = split_heads(key, heads)
    value_heads = split_heads(value, heads)
    row_max = jnp.full((heads, row_count), NEGATIVE, jnp.float32)
    weighted = jnp.zeros((row_count, heads, head_size), jnp.float32)
    piece_keys = lax.all_gather(key, "ctx", axis=0, tiled=True)
    piece_values = lax.all_gather(value, "ctx", axis=0, tiled=True)
    piece_rows = piece_keys.shape[0]
    piece_segment = layout(seq_lengths, jnp.arange(piece_rows, dtype=jnp.int32))[0]
    scaled = (
        jnp.einsum(
            "qhd,khd->hqk",
            query_heads,
            split_heads(piece_keys, heads),
            preferred_element_type=jnp.float32,
        )
        * scale
    )
    matches = (segment[:, None] == piece_segment[None, :])[None]
    masked = jnp.where(matches, scaled, NEGATIVE)
    new_max = jnp.maximum(row_max, jnp.max(masked, axis=2))
    weights_now = jnp.where(matches, jnp.exp(masked - new_max[:, :, None]), 0.0)
    decay = jnp.exp(row_max - new_max)
    row_sum = jnp.sum(weights_now, axis=2)
    partial_value = jnp.einsum(
        "hqk,khd->qhd",
        weights_now.astype(jnp.bfloat16),
        split_heads(piece_values, heads),
        preferred_element_type=jnp.float32,
    )
    weighted = weighted * decay.T[:, :, None] + partial_value
    row_max, row_sum, weighted = (new_max, row_sum, weighted)
    attended_heads = weighted / row_sum.T[:, :, None]
    log_total = row_max + jnp.log(row_sum)
    attended_b = attended_heads.reshape(row_count, width).astype(jnp.bfloat16)
    resid = inputs + jnp.dot(attended_b, full_out, preferred_element_type=jnp.float32)
    norm_two, pull_two = jax.vjp(affine, resid, gain_second, bias_second)
    norm_two_b = norm_two.astype(jnp.bfloat16)
    pre = jnp.dot(norm_two_b, full_up, preferred_element_type=jnp.float32) + bias_hidden
    act, pull_act = jax.vjp(gelu_exact, pre)
    act_b = act.astype(jnp.bfloat16)
    branch = jnp.dot(act_b, full_down, preferred_element_type=jnp.float32) + bias_output
    output = (live[:, None] * (resid + branch)).astype(jnp.bfloat16)
    again = (
        lax.all_gather(w_qkv, "fsdp", axis=0, tiled=True),
        lax.all_gather(w_out, "fsdp", axis=0, tiled=True),
        lax.all_gather(w_up, "fsdp", axis=0, tiled=True),
        lax.all_gather(w_down, "fsdp", axis=0, tiled=True),
        lax.all_gather(w_time, "fsdp", axis=0, tiled=True),
        lax.all_gather(gain_one, "fsdp", axis=0, tiled=True),
        lax.all_gather(bias_one, "fsdp", axis=0, tiled=True),
        lax.all_gather(gain_two, "fsdp", axis=0, tiled=True),
        lax.all_gather(bias_two, "fsdp", axis=0, tiled=True),
        lax.all_gather(bias_up, "fsdp", axis=0, tiled=True),
        lax.all_gather(bias_down, "fsdp", axis=0, tiled=True),
    )
    back_qkv, back_out, back_up, back_down = (again[0], again[1], again[2], again[3])
    grad_y = cotangent[0].astype(jnp.float32) * live[:, None]
    grad_bias_down = jnp.sum(grad_y, axis=0)
    grad_y_b = grad_y.astype(jnp.bfloat16)
    grad_down = contract_rows(act_b, grad_y_b)
    grad_act = contract_cols(grad_y_b, back_down)
    grad_pre = pull_act(grad_act)[0]
    grad_bias_up = jnp.sum(grad_pre, axis=0)
    grad_pre_b = grad_pre.astype(jnp.bfloat16)
    grad_up = contract_rows(norm_two_b, grad_pre_b)
    grad_norm_two = contract_cols(grad_pre_b, back_up)
    grad_resid_norm, grad_gain_two, grad_bias_two = pull_two(grad_norm_two)
    grad_resid = grad_y + grad_resid_norm
    grad_resid_b = grad_resid.astype(jnp.bfloat16)
    grad_out = contract_rows(attended_b, grad_resid_b)
    grad_att = contract_cols(grad_resid_b, back_out).astype(jnp.bfloat16)
    grad_att_heads = split_heads(grad_att, heads)
    delta = jnp.einsum(
        "qhd,qhd->hq", grad_att_heads.astype(jnp.float32), attended_heads, precision=HIGH
    )
    piece_keys = lax.all_gather(key, "ctx", axis=0, tiled=True)
    piece_values = lax.all_gather(value, "ctx", axis=0, tiled=True)
    piece_rows = piece_keys.shape[0]
    piece_segment = layout(seq_lengths, jnp.arange(piece_rows, dtype=jnp.int32))[0]
    keys_split = split_heads(piece_keys, heads)
    scaled = (
        jnp.einsum("qhd,khd->hqk", query_heads, keys_split, preferred_element_type=jnp.float32)
        * scale
    )
    matches = (segment[:, None] == piece_segment[None, :])[None]
    prob = jnp.where(matches, jnp.exp(scaled - log_total[:, :, None]), 0.0)
    grad_prob = jnp.einsum(
        "qhd,khd->hqk",
        grad_att_heads,
        split_heads(piece_values, heads),
        preferred_element_type=jnp.float32,
    )
    grad_score = (prob * (grad_prob - delta[:, :, None])).astype(jnp.bfloat16)
    grad_query = (
        jnp.einsum("hqk,khd->qhd", grad_score, keys_split, preferred_element_type=jnp.float32)
        * scale
    )
    stats_max, stats_delta = (
        lax.all_gather(log_total.T, "ctx", axis=0, tiled=True),
        lax.all_gather(delta.T, "ctx", axis=0, tiled=True),
    )
    piece_queries = lax.all_gather(query, "ctx", axis=0, tiled=True)
    piece_grads = lax.all_gather(grad_att, "ctx", axis=0, tiled=True)
    piece_rows = piece_queries.shape[0]
    piece_segment = layout(seq_lengths, jnp.arange(piece_rows, dtype=jnp.int32))[0]
    queries_split = split_heads(piece_queries, heads)
    grads_split = split_heads(piece_grads, heads)
    scaled = (
        jnp.einsum("qhd,khd->hqk", queries_split, key_heads, preferred_element_type=jnp.float32)
        * scale
    )
    matches = (piece_segment[:, None] == segment[None, :])[None]
    prob = jnp.where(matches, jnp.exp(scaled - stats_max.T[:, :, None]), 0.0)
    grad_value_now = jnp.einsum(
        "hqk,qhd->khd", prob.astype(jnp.bfloat16), grads_split, preferred_element_type=jnp.float32
    )
    grad_prob = jnp.einsum(
        "qhd,khd->hqk", grads_split, value_heads, preferred_element_type=jnp.float32
    )
    grad_score = (prob * (grad_prob - stats_delta.T[:, :, None])).astype(jnp.bfloat16)
    grad_key_now = (
        jnp.einsum("hqk,qhd->khd", grad_score, queries_split, preferred_element_type=jnp.float32)
        * scale
    )
    grad_turned = pull_turn(
        (grad_query.reshape(row_count, width), grad_key_now.reshape(row_count, width))
    )
    grad_mixed_b = jnp.concatenate(
        [grad_turned[0], grad_turned[1], grad_value_now.reshape(row_count, width)], axis=1
    ).astype(jnp.bfloat16)
    grad_qkv = contract_rows(norm_one_b, grad_mixed_b)
    grad_norm_one = contract_cols(grad_mixed_b, back_qkv)
    grad_inputs_norm, grad_gain_one, grad_bias_one, grad_film_tok = pull_one(grad_norm_one)
    grad_tokens = (grad_resid + grad_inputs_norm).astype(jnp.bfloat16)
    grad_film = lax.dot_general(
        onehot_float, grad_film_tok, (((0,), (0,)), ((), ())), precision=HIGH
    )[:seq_count]
    grad_time = lax.dot_general(
        temb.astype(jnp.float32), grad_film, (((0,), (0,)), ((), ())), precision=HIGH
    )
    shares = (
        lax.psum_scatter(
            grad_qkv.astype(jnp.bfloat16), "fsdp", scatter_dimension=0, tiled=True
        ).astype(jnp.float32),
        lax.psum_scatter(
            grad_out.astype(jnp.bfloat16), "fsdp", scatter_dimension=0, tiled=True
        ).astype(jnp.float32),
        lax.psum_scatter(
            grad_up.astype(jnp.bfloat16), "fsdp", scatter_dimension=0, tiled=True
        ).astype(jnp.float32),
        lax.psum_scatter(
            grad_down.astype(jnp.bfloat16), "fsdp", scatter_dimension=0, tiled=True
        ).astype(jnp.float32),
        lax.psum_scatter(
            grad_time.astype(jnp.bfloat16), "fsdp", scatter_dimension=0, tiled=True
        ).astype(jnp.float32),
        lax.psum_scatter(
            grad_gain_one.astype(jnp.bfloat16), "fsdp", scatter_dimension=0, tiled=True
        ).astype(jnp.float32),
        lax.psum_scatter(
            grad_bias_one.astype(jnp.bfloat16), "fsdp", scatter_dimension=0, tiled=True
        ).astype(jnp.float32),
        lax.psum_scatter(
            grad_gain_two.astype(jnp.bfloat16), "fsdp", scatter_dimension=0, tiled=True
        ).astype(jnp.float32),
        lax.psum_scatter(
            grad_bias_two.astype(jnp.bfloat16), "fsdp", scatter_dimension=0, tiled=True
        ).astype(jnp.float32),
        lax.psum_scatter(
            grad_bias_up.astype(jnp.bfloat16), "fsdp", scatter_dimension=0, tiled=True
        ).astype(jnp.float32),
        lax.psum_scatter(
            grad_bias_down.astype(jnp.bfloat16), "fsdp", scatter_dimension=0, tiled=True
        ).astype(jnp.float32),
    )
    (
        share_qkv,
        share_out,
        share_up,
        share_down,
        share_time,
        share_gone,
        share_bone,
        share_gtwo,
        share_btwo,
        share_bup,
        share_bdown,
    ) = shares
    totals = (
        lax.psum(share_qkv.astype(jnp.bfloat16), "ctx").astype(jnp.float32),
        lax.psum(share_out.astype(jnp.bfloat16), "ctx").astype(jnp.float32),
        lax.psum(share_up.astype(jnp.bfloat16), "ctx").astype(jnp.float32),
        lax.psum(share_down.astype(jnp.bfloat16), "ctx").astype(jnp.float32),
        lax.psum(share_time.astype(jnp.bfloat16), "ctx").astype(jnp.float32),
        lax.psum(share_gone.astype(jnp.bfloat16), "ctx").astype(jnp.float32),
        lax.psum(share_bone.astype(jnp.bfloat16), "ctx").astype(jnp.float32),
        lax.psum(share_gtwo.astype(jnp.bfloat16), "ctx").astype(jnp.float32),
        lax.psum(share_btwo.astype(jnp.bfloat16), "ctx").astype(jnp.float32),
        lax.psum(share_bup.astype(jnp.bfloat16), "ctx").astype(jnp.float32),
        lax.psum(share_bdown.astype(jnp.bfloat16), "ctx").astype(jnp.float32),
    )
    return (
        output[None],
        grad_tokens[None],
        totals[0],
        totals[1],
        totals[2],
        totals[3],
        totals[4],
        totals[5],
        totals[6],
        totals[7],
        totals[8],
        totals[9],
        totals[10],
    )


def solution(mesh):
    in_specs = (
        P("fsdp", "ctx", None),
        P("fsdp", None),
        P("fsdp", None),
        P("fsdp", None),
        P("fsdp", None),
        P("fsdp", None),
        P("fsdp"),
        P("fsdp"),
        P("fsdp"),
        P("fsdp"),
        P("fsdp"),
        P("fsdp"),
        P("fsdp", None),
        P("fsdp", None),
        P("fsdp", "ctx", None),
    )
    out_specs = (
        P("fsdp", "ctx", None),
        P("fsdp", "ctx", None),
        P("fsdp", None),
        P("fsdp", None),
        P("fsdp", None),
        P("fsdp", None),
        P("fsdp", None),
        P("fsdp"),
        P("fsdp"),
        P("fsdp"),
        P("fsdp"),
        P("fsdp"),
        P("fsdp"),
    )
    return jax.shard_map(body, mesh=mesh, in_specs=in_specs, out_specs=out_specs, check_vma=False)
```

profile of v0, /device:TPU:0, one launch (start us, length us, event | category | flops | bytes accessed | tf_op | source)
XLA Modules:
  0.0 1203.2 jit_solution(12869326752963828979)
XLA Ops:
  22.1 11.5 all-gather.15.cloned.1.call-done
  36.0 79.6 %all-gather.17.cloned.1.call-done = bf16[1024,3072]{1,0:T(8,128)(2,1)} async-done(((bf16[512,3072]{1,0:T(8,128)(2,1)}), bf16[1024,3072]{1,0:T(8,128)(2,1)}) %all-gather.17.cloned.1.call-update) | async-done | bytes 6291472 | tf_op jit(solution)/shard_map/all_gather | solution.py:97
  145.0 35.7 %all-gather.19.cloned.1.call-done = bf16[2048,1024]{0,1:T(8,128)(2,1)} async-done(((bf16[128,1024]{0,1:T(8,128)(2,1)}), bf16[2048,1024]{0,1:T(8,128)(2,1)}) %all-gather.19.cloned.1.call-update) | async-done | bytes 4194320 | tf_op jit(solution)/shard_map/all_gather | solution.py:154
  191.5 40.6 %all-gather.21.cloned.1.call-done = bf16[2048,1024]{1,0:T(8,128)(2,1)} async-done(((bf16[128,1024]{1,0:T(8,128)(2,1)}), bf16[2048,1024]{1,0:T(8,128)(2,1)}) %all-gather.21.cloned.1.call-update) | async-done | bytes 4194320 | tf_op jit(solution)/shard_map/all_gather | solution.py:155
  232.0 6.4 copy.54
  238.5 13.3 %fusion.100 = (bf16[128,16,64]{0,2,1:T(8,128)(2,1)S(1)}, f32[128,16,64]{0,2,1:T(8,128)}) fusion(f32[128,16]{0,1:T(8,128)S(1)} %bitcast.186, bf16[2048,16,64]{0,2,1:T(8,128)(2,1)} %bitcast.155, f32[16,128,2048]{2,1,0:T(8,128)} %copy-done, f32[16,128]{1,0:T(8,128)S(1)} %broadcast_maximum_fusion, pred[128,2048]{1,0:T(8,128)(4,1)S(1)} %broadcast_compare_fusion.1, ...), kind=kOutput, calls=%fused_computation.164 | convolution fusion | flops 558235648 | bytes 22044672 | tf_op jit(solution)/shard_map/hqk,khd->qhd/dot_general | solution.py:173
  251.8 13.3 %all-gather.23.cloned.1.call-done = bf16[1024,1024]{1,0:T(8,128)(2,1)} async-done(((bf16[512,1024]{1,0:T(8,128)(2,1)}), bf16[1024,1024]{1,0:T(8,128)(2,1)}) %all-gather.23.cloned.1.call-update) | async-done | bytes 2097168 | tf_op jit(solution)/shard_map/all_gather | solution.py:98
  267.4 103.1 %all-gather.25.cloned.1.call-done = bf16[1024,4096]{1,0:T(8,128)(2,1)} async-done(((bf16[512,4096]{1,0:T(8,128)(2,1)}), bf16[1024,4096]{1,0:T(8,128)(2,1)}) %all-gather.25.cloned.1.call-update) | async-done | bytes 8388624 | tf_op jit(solution)/shard_map/all_gather | solution.py:99
  370.5 9.1 multiply_convert_fusion.5
  379.6 96.5 %all-gather.27.cloned.1.call-done = bf16[4096,1024]{1,0:T(8,128)(2,1)} async-done(((bf16[2048,1024]{1,0:T(8,128)(2,1)}), bf16[4096,1024]{1,0:T(8,128)(2,1)}) %all-gather.27.cloned.1.call-update) | async-done | bytes 8388624 | tf_op jit(solution)/shard_map/all_gather | solution.py:100
  476.1 10.8 fusion.102
  499.8 23.5 %all_gather.71 = f32[2048,16]{0,1:T(8,128)} all-gather(f32[128,16]{0,1:T(8,128)S(1)} %get-tuple-element.63), channel_id=1, replica_groups=mesh['ctx'=16,'fsdp'=2] {'ctx'}, dimensions={0}, use_global_device_ids=true | all-gather | bytes 139264 | tf_op jit(solution)/shard_map/all_gather | solution.py:248
  524.5 19.3 %all_gather.73 = f32[2048,16]{0,1:T(8,128)} all-gather(f32[128,16]{0,1:T(8,128)S(1)} %bitcast.191), channel_id=1, replica_groups=mesh['ctx'=16,'fsdp'=2] {'ctx'}, dimensions={0}, use_global_device_ids=true | all-gather | bytes 139264 | tf_op jit(solution)/shard_map/all_gather | solution.py:249
  546.9 10.5 fusion.105
  557.4 14.4 %fusion.26 = f32[16,64,128]{2,1,0:T(8,128)} fusion(bf16[2048,16,64]{0,2,1:T(8,128)(2,1)} %bitcast.154, f32[16,128,2048]{2,1,0:T(8,128)} %copy-done, f32[16,128]{1,0:T(8,128)S(1)} %fusion.59, f32[16,128]{1,0:T(8,128)S(1)} %log_add_fusion, pred[128,2048]{1,0:T(8,128)(4,1)S(1)} %broadcast_compare_fusion.1, bf16[128,16,64]{0,2,1:T(8,128)(2,1)} %bitcast.166, ...), kind=kOutput, calls=%fused_computation.43 | convolution fusion | flops 1099038720 | bytes 26230784 | tf_op jit(solution)/shard_map/hqk,khd->qhd/dot_general | solution.py:244
  571.9 11.9 all-gather.31.cloned.1.call-done
  590.3 15.3 %multiply_convert_fusion.12 = bf16[16,2048,128]{2,1,0:T(8,128)(2,1)S(1)} fusion(f32[16,2048,128]{2,1,0:T(8,128)} %fusion.105, f32[16,2048]{1,0:T(8,128)} %bitcast.183, f32[16,2048]{1,0:T(8,128)S(1)} %bitcast.181, pred[2048,128]{1,0:T(8,128)(4,1)S(1)} %copy-done.23, bf16[2048,16,64]{0,2,1:T(8,128)(2,1)} %bitcast.157, ...), kind=kOutput, calls=%fused_computation.clone.clone.clone.clone.1 | convolution fusion | flops 562036736 | bytes 30146560 | tf_op jit(solution)/shard_map/qhd,khd->hqk/dot_general | solution.py:266
  608.6 11.1 fusion.34
  644.2 102.0 %reduce-scatter.10.cloned.1.call-done = bf16[512,4096]{1,0:T(8,128)(2,1)} async-done(((bf16[1024,4096]{1,0:T(8,128)(2,1)}), bf16[512,4096]{1,0:T(8,128)(2,1)}) %reduce-scatter.10.cloned.1.call-update) | async-done | bytes 4194320 | tf_op jit(solution)/shard_map/reduce_scatter | solution.py:297
  746.2 102.2 %reduce-scatter.12.cloned.1.call-done = bf16[2048,1024]{1,0:T(8,128)(2,1)} async-done(((bf16[4096,1024]{1,0:T(8,128)(2,1)}), bf16[2048,1024]{1,0:T(8,128)(2,1)}) %reduce-scatter.12.cloned.1.call-update) | async-done | bytes 4194320 | tf_op jit(solution)/shard_map/reduce_scatter | solution.py:300
  848.4 79.8 %reduce-scatter.6.cloned.1.call-done = bf16[512,3072]{1,0:T(8,128)(2,1)} async-done(((bf16[1024,3072]{1,0:T(8,128)(2,1)}), bf16[512,3072]{1,0:T(8,128)(2,1)}) %reduce-scatter.6.cloned.1.call-update) | async-done | bytes 3145744 | tf_op jit(solution)/shard_map/reduce_scatter | solution.py:291
  940.7 7.1 all-reduce.15
  948.2 35.4 %all-reduce.13 = (bf16[512]{0:T(512)(128)(2,1)S(1)}, bf16[512]{0:T(512)(128)(2,1)S(1)}, bf16[512]{0:T(512)(128)(2,1)S(1)}, bf16[512]{0:T(512)(128)(2,1)S(1)}, bf...) all-reduce(bf16[512]{0:T(512)(128)(2,1)S(1)} %dynamic-slice.1, ...), channel_id=1, replica_groups=mesh['ctx'=16,'fsdp'=2] {'ctx'}, use_global_device_ids=true, to_apply=%region_23.24 | all-reduce | flops 4608 | bytes 18432 | tf_op jit(solution)/shard_map/psum | solution.py:344
  988.0 191.4 %all-reduce.18.cloned.1.call-done = (bf16[512,3072]{1,0:T(8,128)(2,1)}, bf16[512,1024]{1,0:T(8,128)(2,1)}, bf16[512,4096]{1,0:T(8,128)(2,1)}, bf16[2048,1024]{1,0:T(8,128)(2,1)}, bf16[128,2048]{1,0:T(8,128)(2,1)}) async-done(((bf16[512,3072]{1,0:T(8,128)(2,1)}, bf16[512,1024]{1,0:T(8,128)(2,1)}, bf16[512,4096]{1,0:T(8,128)(2,1)}, bf16[2048,1024]{1,0:T(8,128)(2,1)}, bf16[128,2048]{1,0:T(8,128)(2,1)}), ...) | async-done | bytes 13107216 | tf_op jit(solution)/shard_map/psum | solution.py:339
  (264 shorter events, 141.8 us)
Async XLA Ops:
  7.2 26.4 %all-gather.15.cloned.1.call-start = ((), (), s32[]{:S(2)}) async-start(), calls=%async_computation.5 | async-start | bytes 1572864 | tf_op jit(solution)/shard_map/all_gather | solution.py:101
  7.9 107.7 %all-gather.17.cloned.1.call-start = ((), (), s32[]{:S(2)}) async-start(), calls=%async_computation.6 | async-start | bytes 9437184 | tf_op jit(solution)/shard_map/all_gather | solution.py:97
  8.7 172.0 %all-gather.19.cloned.1.call-start = ((), (), s32[]{:S(2)}) async-start(), calls=%async_computation.7 | async-start | bytes 4456448 | tf_op jit(solution)/shard_map/all_gather | solution.py:154
  21.1 98.3 %copy-start.47 = (f32[128]{0:T(128)}, f32[128]{0:T(128)S(1)}, u32[]{:S(2)}) copy-start(f32[128]{0:T(128)S(1)} %broadcast_multiply_fusion.1) | copy-start | bytes 1540
  21.3 98.1 %copy-start.53 = (f32[128]{0:T(128)}, f32[128]{0:T(128)S(1)}, u32[]{:S(2)}) copy-start(f32[128]{0:T(128)S(1)} %fusion.78) | copy-start | bytes 1540
  22.1 102.4 %copy-start.27 = (f32[128,32]{0,1:T(8,128)}, f32[128,32]{0,1:T(8,128)S(1)}, u32[]{:S(2)}) copy-start(f32[128,32]{0,1:T(8,128)S(1)} %get-tuple-element.65) | copy-start | bytes 49156
  127.3 104.7 %all-gather.21.cloned.1.call-start = ((), (), s32[]{:S(2)}) async-start(), calls=%async_computation.8 | async-start | bytes 4456448 | tf_op jit(solution)/shard_map/all_gather | solution.py:155
  128.1 137.0 %all-gather.23.cloned.1.call-start = ((), (), s32[]{:S(2)}) async-start(), calls=%async_computation.9 | async-start | bytes 3145728 | tf_op jit(solution)/shard_map/all_gather | solution.py:98
  128.7 241.8 %all-gather.25.cloned.1.call-start = ((), (), s32[]{:S(2)}) async-start(), calls=%async_computation.10 | async-start | bytes 12582912 | tf_op jit(solution)/shard_map/all_gather | solution.py:99
  129.3 346.8 %all-gather.27.cloned.1.call-start = ((), (), s32[]{:S(2)}) async-start(), calls=%async_computation.11 | async-start | bytes 12582912 | tf_op jit(solution)/shard_map/all_gather | solution.py:100
  130.1 416.8 %all-gather.29.cloned.1.call-start = ((), (), s32[]{:S(2)}) async-start(), calls=%async_computation.12 | async-start | bytes 4456448 | tf_op jit(solution)/shard_map/all_gather | solution.py:251
  144.8 439.0 %all-gather.31.cloned.1.call-start = ((), (), s32[]{:S(2)}) async-start(), calls=%async_computation.13 | async-start | bytes 4456448 | tf_op jit(solution)/shard_map/all_gather | solution.py:252
  251.8 118.7 %copy-start.17 = (bf16[128,16,64]{0,2,1:T(8,128)(2,1)}, bf16[128,16,64]{0,2,1:T(8,128)(2,1)S(1)}, u32[]{:S(2)}) copy-start(bf16[128,16,64]{0,2,1:T(8,128)(2,1)S(1)} %get-tuple-element.69) | copy-start | bytes 786436
  251.8 118.7 %copy-start.33 = (f32[4096]{0:T(1024)S(1)}, f32[4096]{0:T(1024)}, u32[]{:S(2)}) copy-start(f32[4096]{0:T(1024)} %convert_element_type.264) | copy-start | bytes 49156
  267.2 223.2 %copy-start.36 = (f32[128]{0:T(128)}, f32[128]{0:T(128)S(1)}, u32[]{:S(2)}) copy-start(f32[128]{0:T(128)S(1)} %broadcast_multiply_fusion) | copy-start | bytes 1540
  267.4 223.0 %copy-start.38 = (f32[128]{0:T(128)}, f32[128]{0:T(128)S(1)}, u32[]{:S(2)}) copy-start(f32[128]{0:T(128)S(1)} %fusion.79) | copy-start | bytes 1540
  370.5 105.6 %copy-start.34 = (f32[128]{0:T(128)S(1)}, f32[128]{0:T(128)}, u32[]{:S(2)}) copy-start(f32[128]{0:T(128)} %get-tuple-element.43) | copy-start | bytes 1540
  494.5 149.0 %reduce-scatter.8.cloned.1.call-start = ((), (), s32[]{:S(2)}) async-start(), calls=%async_computation.15 | async-start | bytes 3145728 | tf_op jit(solution)/shard_map/reduce_scatter | solution.py:294
  571.9 72.3 %reduce-scatter.14.cloned.1.call-start = ((), (), s32[]{:S(2)}) async-start(), calls=%async_computation.18 | async-start | bytes 1572864 | tf_op jit(solution)/shard_map/reduce_scatter | solution.py:303
  625.0 121.2 %reduce-scatter.10.cloned.1.call-start = ((), (), s32[]{:S(2)}) async-start(), calls=%async_computation.16 | async-start | bytes 12582912 | tf_op jit(solution)/shard_map/reduce_scatter | solution.py:297
  631.2 217.2 %reduce-scatter.12.cloned.1.call-start = ((), (), s32[]{:S(2)}) async-start(), calls=%async_computation.17 | async-start | bytes 12582912 | tf_op jit(solution)/shard_map/reduce_scatter | solution.py:300
  637.9 290.3 %reduce-scatter.6.cloned.1.call-start = ((), (), s32[]{:S(2)}) async-start(), calls=%async_computation.14 | async-start | bytes 9437184 | tf_op jit(solution)/shard_map/reduce_scatter | solution.py:291
  643.5 535.9 %all-reduce.18.cloned.1.call-start = ((), (), s32[]{:S(2)}) async-start(), calls=%async_computation.19 | async-start | bytes 26214400 | tf_op jit(solution)/shard_map/psum | solution.py:339
  935.2 51.9 %copy-start.6 = (f32[128,1024]{1,0:T(8,128)S(1)}, f32[128,1024]{1,0:T(8,128)}, u32[]{:S(2)}) copy-start(f32[128,1024]{1,0:T(8,128)} %copy-done.5) | copy-start | bytes 1572868
  (57 other events, 434.5 us)
Sparse Core Ops, SparseCore 0:
  9.6 23.9 all-gather.14
  35.2 80.4 all-gather.16
  127.4 53.2 all-gather.18
  183.3 48.7 all-gather.20
  233.4 31.5 all-gather.22
  266.5 103.9 all-gather.24
  372.0 103.9 all-gather.26
  478.8 54.0 all-gather.28
  535.0 48.7 all-gather.30
  586.5 30.2 reduce-scatter.7
  625.1 18.9 reduce-scatter.13
  646.9 99.2 reduce-scatter.9
  749.1 99.2 reduce-scatter.11
  851.1 77.0 reduce-scatter.5
  933.9 245.5 all-reduce.17
where the time goes:
time: 1210 us; the launch traced here: 1200 us
  waiting for transfers between devices  872 us (72%)
  matrix products  132 us (11%)
  blocking collectives  112 us (9%)
  other arithmetic  40 us (3%)
  local copies, waits for them, and re-layouts  29.2 us (2%)
  between operations  17.5 us (1%)
    psum x1, waiting for transfers between devices, body(): lax.psum(share_qkv.astype(jnp.bfloat16), 'ctx').astype(jnp.float32)  191 us
    all_gather x1, waiting for transfers between devices, body(): lax.all_gather(w_up, 'fsdp', axis=0, tiled=True)  103 us
    reduce_scatter x1, waiting for transfers between devices, body(): lax.psum_scatter(grad_down.astype(jnp.bfloat16), 'fsdp', scatter_dimensio...  102 us
    reduce_scatter x1, waiting for transfers between devices, body(): lax.psum_scatter(grad_up.astype(jnp.bfloat16), 'fsdp', scatter_dimension=...  102 us
    all_gather x1, waiting for transfers between devices, body(): lax.all_gather(w_down, 'fsdp', axis=0, tiled=True)  96.5 us
    reduce_scatter x1, waiting for transfers between devices, body(): lax.psum_scatter(grad_qkv.astype(jnp.bfloat16), 'fsdp', scatter_dimension...  79.8 us
    all_gather x1, waiting for transfers between devices, body(): lax.all_gather(w_qkv, 'fsdp', axis=0, tiled=True)  79.6 us
    all_gather x1, waiting for transfers between devices, body(): piece_values = lax.all_gather(value, 'ctx', axis=0, tiled=True)  40.6 us
  transfers between devices with their start and end apart: 15, of which 13 were waited for; matrix products, arithmetic and copies ran while one was open for 14% of the time, Pallas kernels for 0%

commit v1 on v0

--- a/solution.py
+++ b/solution.py
@@ -151,8 +151,11 @@
     value_heads = split_heads(value, heads)
     row_max = jnp.full((heads, row_count), NEGATIVE, jnp.float32)
     weighted = jnp.zeros((row_count, heads, head_size), jnp.float32)
-    piece_keys = lax.all_gather(key, "ctx", axis=0, tiled=True)
-    piece_values = lax.all_gather(value, "ctx", axis=0, tiled=True)
+    piece_keys, piece_values = jnp.split(
+        lax.all_gather(jnp.concatenate([key, value], axis=1), "ctx", axis=0, tiled=True),
+        [key.shape[1]],
+        axis=1,
+    )
     piece_rows = piece_keys.shape[0]
     piece_segment = layout(seq_lengths, jnp.arange(piece_rows, dtype=jnp.int32))[0]
     scaled = (

time: 1210 us -> 1290 us (1.066)
  waiting for transfers between devices: 872 us -> 946 us
  local copies, waits for them, and re-layouts: 29.2 us -> 45.2 us
    all_gather x0 -> x1, waiting for transfers between devices: none -> 57.4 us  [body(): lax.all_gather(jnp.concatenate([key, value], axis=1), 'ctx', axis=0, tile...]
    all_gather x1, waiting for transfers between devices: 0.01 us -> 43.7 us  [body(): piece_queries = lax.all_gather(query, 'ctx', axis=0, tiled=True)]
    split x0 -> x3, local copies, waits for them, and re-layouts: none -> 19 us  [body(): jnp.split(lax.all_gather(jnp.concatenate([key, value], axis=1), 'ctx', ax...]
    all_gather x1, waiting for transfers between devices: 13.3 us -> 0.01 us  [body(): lax.all_gather(w_out, 'fsdp', axis=0, tiled=True)]
  transfers between devices with their start and end apart: 15 -> 16, of which waited for: 13 -> 12; matrix products, arithmetic and copies ran while one was open for 14% -> 14% of each run, Pallas kernels for 0% -> 0%
where the time goes in v1:
time: 1290 us
  waiting for transfers between devices  946 us (73%)
  matrix products  135 us (10%)
  blocking collectives  110 us (9%)
  local copies, waits for them, and re-layouts  45.2 us (4%)
  other arithmetic  33.2 us (3%)
  between operations  17.5 us (1%)
    psum x1, waiting for transfers between devices, body(): lax.psum(share_qkv.astype(jnp.bfloat16), 'ctx').astype(jnp.float32)  191 us
    reduce_scatter x1, waiting for transfers between devices, body(): lax.psum_scatter(grad_down.astype(jnp.bfloat16), 'fsdp', scatter_dimensio...  102 us
    reduce_scatter x1, waiting for transfers between devices, body(): lax.psum_scatter(grad_up.astype(jnp.bfloat16), 'fsdp', scatter_dimension=...  101 us
    all_gather x1, waiting for transfers between devices, body(): lax.all_gather(w_down, 'fsdp', axis=0, tiled=True)  96.3 us
    all_gather x1, waiting for transfers between devices, body(): lax.all_gather(w_up, 'fsdp', axis=0, tiled=True)  95 us
    reduce_scatter x1, waiting for transfers between devices, body(): lax.psum_scatter(grad_qkv.astype(jnp.bfloat16), 'fsdp', scatter_dimension...  79.8 us
    all_gather x1, waiting for transfers between devices, body(): lax.all_gather(w_qkv, 'fsdp', axis=0, tiled=True)  79.6 us
    all_gather x1, waiting for transfers between devices, body(): lax.all_gather(jnp.concatenate([key, value], axis=1), 'ctx', axis=0, tile...  57.4 us
  transfers between devices with their start and end apart: 16, of which 12 were waited for; matrix products, arithmetic and copies ran while one was open for 14% of the time, Pallas kernels for 0%

profile of v1, /device:TPU:0, one launch (start us, length us, event | category | flops | bytes accessed | tf_op | source)
XLA Modules:
  0.0 1287.6 jit_solution(13263683324789213824)
XLA Ops:
  20.4 13.2 %all-gather.16.cloned.1.call-done = bf16[256,2048]{1,0:T(8,128)(2,1)} async-done(((bf16[128,2048]{1,0:T(8,128)(2,1)}), bf16[256,2048]{1,0:T(8,128)(2,1)}) %all-gather.16.cloned.1.call-update) | async-done | bytes 1048592 | tf_op jit(solution)/shard_map/all_gather | solution.py:101
  36.0 79.6 %all-gather.18.cloned.1.call-done = bf16[1024,3072]{1,0:T(8,128)(2,1)} async-done(((bf16[512,3072]{1,0:T(8,128)(2,1)}), bf16[1024,3072]{1,0:T(8,128)(2,1)}) %all-gather.18.cloned.1.call-update) | async-done | bytes 6291472 | tf_op jit(solution)/shard_map/all_gather | solution.py:97
  141.8 57.4 %all-gather.20.cloned.1.call-done = bf16[2048,2048]{1,0:T(8,128)(2,1)} async-done(((bf16[128,2048]{1,0:T(8,128)(2,1)}), bf16[2048,2048]{1,0:T(8,128)(2,1)}) %all-gather.20.cloned.1.call-update) | async-done | bytes 8388624 | tf_op jit(solution)/shard_map/all_gather | solution.py:155
  230.2 9.4 fusion.102
  242.4 95.0 %all-gather.24.cloned.1.call-done = bf16[1024,4096]{1,0:T(8,128)(2,1)} async-done(((bf16[512,4096]{1,0:T(8,128)(2,1)}), bf16[1024,4096]{1,0:T(8,128)(2,1)}) %all-gather.24.cloned.1.call-update) | async-done | bytes 8388624 | tf_op jit(solution)/shard_map/all_gather | solution.py:99
  337.4 9.1 multiply_convert_fusion.5
  346.6 96.3 %all-gather.26.cloned.1.call-done = bf16[4096,1024]{1,0:T(8,128)(2,1)} async-done(((bf16[2048,1024]{1,0:T(8,128)(2,1)}), bf16[4096,1024]{1,0:T(8,128)(2,1)}) %all-gather.26.cloned.1.call-update) | async-done | bytes 8388624 | tf_op jit(solution)/shard_map/all_gather | solution.py:100
  442.9 10.1 fusion.104
  461.6 34.0 %all-gather.30.cloned.1.call-done = bf16[2048,1024]{1,0:T(8,128)(2,1)} async-done(((bf16[128,1024]{1,0:T(8,128)(2,1)}), bf16[2048,1024]{1,0:T(8,128)(2,1)}) %all-gather.30.cloned.1.call-update) | async-done | bytes 4194320 | tf_op jit(solution)/shard_map/all_gather | solution.py:229
  502.1 47.5 %all-gather.28.cloned.1.call-done = bf16[2048,1024]{0,1:T(8,128)(2,1)} async-done(((bf16[128,1024]{0,1:T(8,128)(2,1)}), bf16[2048,1024]{0,1:T(8,128)(2,1)}) %all-gather.28.cloned.1.call-update) | async-done | bytes 4194320 | tf_op jit(solution)/shard_map/all_gather | solution.py:228
  549.6 10.4 fusion.107
  560.0 43.7 %all-gather.32.cloned.1.call-done = bf16[2048,1024]{0,1:T(8,128)(2,1)} async-done(((bf16[128,1024]{0,1:T(8,128)(2,1)}), bf16[2048,1024]{0,1:T(8,128)(2,1)}) %all-gather.32.cloned.1.call-update) | async-done | bytes 4194320 | tf_op jit(solution)/shard_map/all_gather | solution.py:254
  603.7 10.6 fusion.108
  614.4 20.4 %all_gather.73 = f32[2048,16]{0,1:T(8,128)} all-gather(f32[128,16]{0,1:T(8,128)S(1)} %get-tuple-element.65), channel_id=1, replica_groups=mesh['ctx'=16,'fsdp'=2] {'ctx'}, dimensions={0}, use_global_device_ids=true | all-gather | bytes 139264 | tf_op jit(solution)/shard_map/all_gather | solution.py:251
  636.0 20.0 %all_gather.75 = f32[2048,16]{0,1:T(8,128)} all-gather(f32[128,16]{0,1:T(8,128)S(1)} %bitcast.200), channel_id=1, replica_groups=mesh['ctx'=16,'fsdp'=2] {'ctx'}, dimensions={0}, use_global_device_ids=true | all-gather | bytes 139264 | tf_op jit(solution)/shard_map/all_gather | solution.py:252
  659.2 14.3 %fusion.27 = f32[16,64,128]{2,1,0:T(8,128)} fusion(bf16[2048,16,64]{0,2,1:T(8,128)(2,1)} %bitcast.161, f32[16,128,2048]{2,1,0:T(8,128)} %fusion.107, f32[16,128]{1,0:T(8,128)S(1)} %fusion.60, f32[16,128]{1,0:T(8,128)S(1)} %log_add_fusion, pred[128,2048]{1,0:T(8,128)(4,1)S(1)} %copy-done.21, bf16[128,16,64]{0,2,1:T(8,128)(2,1)S(1)} %bitcast.175, ...), kind=kOutput, calls=%fused_computation.44 | convolution fusion | flops 1099038720 | bytes 26230784 | tf_op jit(solution)/shard_map/hqk,khd->qhd/dot_general | solution.py:247
  680.1 16.3 %multiply_convert_fusion.12 = bf16[16,2048,128]{2,1,0:T(8,128)(2,1)S(1)} fusion(f32[16,2048,128]{2,1,0:T(8,128)} %fusion.108, f32[16,2048]{1,0:T(8,128)} %bitcast.192, f32[16,2048]{1,0:T(8,128)} %bitcast.190, pred[2048,128]{1,0:T(8,128)(4,1)S(1)} %copy-done.34, bf16[2048,16,64]{0,2,1:T(8,128)(2,1)} %bitcast.166, ...), kind=kOutput, calls=%fused_computation.clone.clone.clone.clone.1 | convolution fusion | flops 562036736 | bytes 30146560 | tf_op jit(solution)/shard_map/qhd,khd->hqk/dot_general | solution.py:269
  699.5 7.4 fusion.35
  730.1 101.4 %reduce-scatter.10.cloned.1.call-done = bf16[512,4096]{1,0:T(8,128)(2,1)} async-done(((bf16[1024,4096]{1,0:T(8,128)(2,1)}), bf16[512,4096]{1,0:T(8,128)(2,1)}) %reduce-scatter.10.cloned.1.call-update) | async-done | bytes 4194320 | tf_op jit(solution)/shard_map/reduce_scatter | solution.py:300
  831.6 102.1 %reduce-scatter.12.cloned.1.call-done = bf16[2048,1024]{1,0:T(8,128)(2,1)} async-done(((bf16[4096,1024]{1,0:T(8,128)(2,1)}), bf16[2048,1024]{1,0:T(8,128)(2,1)}) %reduce-scatter.12.cloned.1.call-update) | async-done | bytes 4194320 | tf_op jit(solution)/shard_map/reduce_scatter | solution.py:303
  933.7 79.8 %reduce-scatter.6.cloned.1.call-done = bf16[512,3072]{1,0:T(8,128)(2,1)} async-done(((bf16[1024,3072]{1,0:T(8,128)(2,1)}), bf16[512,3072]{1,0:T(8,128)(2,1)}) %reduce-scatter.6.cloned.1.call-update) | async-done | bytes 3145744 | tf_op jit(solution)/shard_map/reduce_scatter | solution.py:294
  1025.8 7.1 all-reduce.15
  1033.3 35.5 %all-reduce.13 = (bf16[512]{0:T(512)(128)(2,1)S(1)}, bf16[512]{0:T(512)(128)(2,1)S(1)}, bf16[512]{0:T(512)(128)(2,1)S(1)}, bf16[512]{0:T(512)(128)(2,1)S(1)}, bf...) all-reduce(bf16[512]{0:T(512)(128)(2,1)S(1)} %dynamic-slice.1, ...), channel_id=1, replica_groups=mesh['ctx'=16,'fsdp'=2] {'ctx'}, use_global_device_ids=true, to_apply=%region_23.24 | all-reduce | flops 4608 | bytes 18432 | tf_op jit(solution)/shard_map/psum | solution.py:347
  1073.1 191.5 %all-reduce.18.cloned.1.call-done = (bf16[512,3072]{1,0:T(8,128)(2,1)}, bf16[512,1024]{1,0:T(8,128)(2,1)}, bf16[512,4096]{1,0:T(8,128)(2,1)}, bf16[2048,1024]{1,0:T(8,128)(2,1)}, bf16[128,2048]{1,0:T(8,128)(2,1)}) async-done(((bf16[512,3072]{1,0:T(8,128)(2,1)}, bf16[512,1024]{1,0:T(8,128)(2,1)}, bf16[512,4096]{1,0:T(8,128)(2,1)}, bf16[2048,1024]{1,0:T(8,128)(2,1)}, bf16[128,2048]{1,0:T(8,128)(2,1)}), ...) | async-done | bytes 13107216 | tf_op jit(solution)/shard_map/psum | solution.py:342
  (248 shorter events, 157.9 us)
Async XLA Ops:
  7.2 26.4 %all-gather.16.cloned.1.call-start = ((), (), s32[]{:S(2)}) async-start(), calls=%async_computation.5 | async-start | bytes 1572864 | tf_op jit(solution)/shard_map/all_gather | solution.py:101
  7.9 107.6 %all-gather.18.cloned.1.call-start = ((), (), s32[]{:S(2)}) async-start(), calls=%async_computation.6 | async-start | bytes 9437184 | tf_op jit(solution)/shard_map/all_gather | solution.py:97
  8.7 190.5 %all-gather.20.cloned.1.call-start = ((), (), s32[]{:S(2)}) async-start(), calls=%async_computation.7 | async-start | bytes 8912896 | tf_op jit(solution)/shard_map/all_gather | solution.py:155
  36.0 83.4 %copy-start.6 = (bf16[128,1024]{1,0:T(8,128)(2,1)}, bf16[128,1024]{1,0:T(8,128)(2,1)S(1)}, u32[]{:S(2)}) copy-start(bf16[128,1024]{1,0:T(8,128)(2,1)S(1)} %fusion.54) | copy-start | bytes 786436
  124.1 115.5 %all-gather.22.cloned.1.call-start = ((), (), s32[]{:S(2)}) async-start(), calls=%async_computation.8 | async-start | bytes 3145728 | tf_op jit(solution)/shard_map/all_gather | solution.py:98
  124.7 212.7 %all-gather.24.cloned.1.call-start = ((), (), s32[]{:S(2)}) async-start(), calls=%async_computation.9 | async-start | bytes 12582912 | tf_op jit(solution)/shard_map/all_gather | solution.py:99
  125.4 317.5 %all-gather.26.cloned.1.call-start = ((), (), s32[]{:S(2)}) async-start(), calls=%async_computation.10 | async-start | bytes 12582912 | tf_op jit(solution)/shard_map/all_gather | solution.py:100
  125.9 369.7 %all-gather.30.cloned.1.call-start = ((), (), s32[]{:S(2)}) async-start(), calls=%async_computation.12 | async-start | bytes 4456448 | tf_op jit(solution)/shard_map/all_gather | solution.py:229
  126.7 422.9 %all-gather.28.cloned.1.call-start = ((), (), s32[]{:S(2)}) async-start(), calls=%async_computation.11 | async-start | bytes 4456448 | tf_op jit(solution)/shard_map/all_gather | solution.py:228
  127.4 476.3 %all-gather.32.cloned.1.call-start = ((), (), s32[]{:S(2)}) async-start(), calls=%async_computation.13 | async-start | bytes 4456448 | tf_op jit(solution)/shard_map/all_gather | solution.py:254
  140.8 89.4 %copy-start.20 = (pred[128,2048]{1,0:T(8,128)(4,1)}, pred[128,2048]{1,0:T(8,128)(4,1)S(1)}, u32[]{:S(2)}) copy-start(pred[128,2048]{1,0:T(8,128)(4,1)S(1)} %broadcast_compare_fusion.1) | copy-start | bytes 786436
  141.6 531.9 %all-gather.34.cloned.1.call-start = ((), (), s32[]{:S(2)}) async-start(), calls=%async_computation.14 | async-start | bytes 4456448 | tf_op jit(solution)/shard_map/all_gather | solution.py:255
  239.6 97.8 %copy-start.28 = (bf16[128,16,64]{0,2,1:T(8,128)(2,1)}, bf16[128,16,64]{0,2,1:T(8,128)(2,1)S(1)}, u32[]{:S(2)}) copy-start(bf16[128,16,64]{0,2,1:T(8,128)(2,1)S(1)} %get-tuple-element.71) | copy-start | bytes 786436
  337.4 105.4 %copy-start.22 = (bf16[1,128,1024]{2,1,0:T(8,128)(2,1)S(1)}, bf16[1,128,1024]{2,1,0:T(8,128)(2,1)}, u32[]{:S(2)}) copy-start(bf16[1,128,1024]{2,1,0:T(8,128)(2,1)} %param.29) | copy-start | bytes 786436
  459.6 270.4 %reduce-scatter.8.cloned.1.call-start = ((), (), s32[]{:S(2)}) async-start(), calls=%async_computation.16 | async-start | bytes 3145728 | tf_op jit(solution)/shard_map/reduce_scatter | solution.py:297
  549.6 54.2 %copy-start.18 = (bf16[128,16,2,32]{0,3,2,1:T(8,128)(2,1)S(1)}, bf16[128,16,2,32]{0,3,2,1:T(8,128)(2,1)}, u32[]{:S(2)}) copy-start(bf16[128,16,2,32]{0,3,2,1:T(8,128)(2,1)} %copy-done.17) | copy-start | bytes 786436
  659.1 71.0 %reduce-scatter.14.cloned.1.call-start = ((), (), s32[]{:S(2)}) async-start(), calls=%async_computation.19 | async-start | bytes 1572864 | tf_op jit(solution)/shard_map/reduce_scatter | solution.py:306
  680.1 18.3 %slice-start.2 = ((s8[16777216]{0:T(1024)(128)(4,1)}), s8[4194304]{0:T(1024)(128)(4,1)S(1)}, s32[]{:S(2)}) async-start(s8[16777216]{0:T(1024)(128)(4,1)} %bitcast.158), calls=%async_computation.23 | async-start | bytes 8388608
  680.1 18.3 %slice-start.3 = ((s8[16777216]{0:T(1024)(128)(4,1)}), s8[4194304]{0:T(1024)(128)(4,1)S(1)}, s32[]{:S(2)}) async-start(s8[16777216]{0:T(1024)(128)(4,1)} %bitcast.158), calls=%async_computation.24 | async-start | bytes 8388608
  711.4 120.1 %reduce-scatter.10.cloned.1.call-start = ((), (), s32[]{:S(2)}) async-start(), calls=%async_computation.17 | async-start | bytes 12582912 | tf_op jit(solution)/shard_map/reduce_scatter | solution.py:300
  717.5 216.1 %reduce-scatter.12.cloned.1.call-start = ((), (), s32[]{:S(2)}) async-start(), calls=%async_computation.18 | async-start | bytes 12582912 | tf_op jit(solution)/shard_map/reduce_scatter | solution.py:303
  724.3 289.2 %reduce-scatter.6.cloned.1.call-start = ((), (), s32[]{:S(2)}) async-start(), calls=%async_computation.15 | async-start | bytes 9437184 | tf_op jit(solution)/shard_map/reduce_scatter | solution.py:294
  730.0 534.6 %all-reduce.18.cloned.1.call-start = ((), (), s32[]{:S(2)}) async-start(), calls=%async_computation.20 | async-start | bytes 26214400 | tf_op jit(solution)/shard_map/psum | solution.py:342
  1020.4 51.9 %copy-start.9 = (f32[128,1024]{1,0:T(8,128)S(1)}, f32[128,1024]{1,0:T(8,128)}, u32[]{:S(2)}) copy-start(f32[128,1024]{1,0:T(8,128)} %copy-done.8) | copy-start | bytes 1572868
  (45 other events, 223.9 us)
Sparse Core Ops, SparseCore 0:
  9.6 23.9 all-gather.15
  35.2 80.3 all-gather.17
  124.3 74.8 all-gather.19
  200.6 31.3 all-gather.21
  233.4 103.9 all-gather.23
  338.8 103.9 all-gather.25
  445.0 50.5 all-gather.29
  497.8 51.6 all-gather.27
  552.3 51.3 all-gather.31
  606.3 50.0 all-gather.33
  659.2 30.3 reduce-scatter.7
  711.5 17.8 reduce-scatter.13
  732.3 99.2 reduce-scatter.9
  834.4 99.2 reduce-scatter.11
  936.4 77.0 reduce-scatter.5
  1019.1 245.4 all-reduce.17
